TPU v7x, 32 devices: a whole 2x2x4 slice. The times are simulated.
32 devices in a mesh: seq: 4 (over y, x), chan: 8 (over z, core).
Axes of the slice: x: 2, y: 2, z: 4, core: 2. Of those that a mesh axis runs over, the one named last changes fastest.
Arguments:
- query_stream: bfloat16 [2048, 8192], P('seq', 'chan'), may hold values from -6 to 6
- key_stream: bfloat16 [2048, 8192], P('seq', 'chan'), may hold values from -6 to 6
- value_stream: bfloat16 [2048, 8192], P('seq', 'chan'), may hold values from -6 to 6
- teacher_filter: float32 [512, 128], P('chan'), may hold values from -0.5 to 0.5
- student_filter: float32 [512, 128], P('chan'), may hold values from -0.5 to 0.5
- group_mask: int32 [512], P('chan'), may hold values 0 or 1
- base_ids: int32 [2048], replicated, may hold values from 0 to 7
- teacher_proj: bfloat16 [8192, 8192], P('chan', 'seq'), may hold values from -0.0625 to 0.0625
- student_proj: bfloat16 [8192, 8192], P('chan', 'seq'), may hold values from -0.09375 to 0.09375
Outputs:
- proj_grad: float32 [8192, 8192], P('chan', 'seq')
All inputs are finite; a program needn't handle non-finite values. No bound on the sum of `group_mask` on one device may be relied on, other than what follows from the above.
Results may differ from a plain program's by a relative error of at most 0.022.
Values may be sent and summed in bfloat16 or wider, within the bound.
A program may use at most 128 MiB of HBM per device.

v0:
```python
import functools

import jax
import jax.numpy as jnp
from jax import lax
from jax.experimental import pallas as pl
from jax.experimental.pallas import tpu as pltpu
from jax.sharding import PartitionSpec as P

repeat_weight = 0.1
lanes = 128
halves = 2
vmem_limit = 66_000_000


def shifted(value, axis, steps):
    count = lax.axis_size(axis)
    initial, last = (max(0, -steps), min(count, count - steps))
    return lax.ppermute(value, axis, [(source, source + steps) for source in range(initial, last)])


def mix_kernel(taps, width, q_ref, k_ref, v_ref, prior_ref, rows_ref, keep_ref, out_ref, ext_ref):
    tokens = q_ref.shape[0]
    blocks = tokens // taps
    group_count = lanes // width
    gated = (k_ref[...].astype(jnp.float32) * v_ref[...].astype(jnp.float32)).astype(jnp.bfloat16)
    ext_ref[0:taps, 0:lanes] = prior_ref[...]
    for block in range(blocks):
        piece = gated[block * taps : (block + 1) * taps]
        ext_ref[taps : 2 * taps, block * lanes : (block + 1) * lanes] = piece
        if block + 1 < blocks:
            ext_ref[0:taps, (block + 1) * lanes : (block + 2) * lanes] = piece
    windows = ext_ref[...]
    lane_group = lax.broadcasted_iota(jnp.int32, (2 * taps, blocks * lanes), 1) % lanes // width
    mixed = jnp.zeros((2 * taps, blocks * lanes), jnp.float32)
    for group in range(group_count):
        tables = []
        for kind in range(2):
            base = jnp.broadcast_to(rows_ref[kind, group : group + 1, :], (taps, 2 * taps))
            tables.append(pltpu.roll(base, 0, 1, stride=1, stride_axis=0))
        table = jnp.concatenate(tables, axis=0).astype(jnp.bfloat16)
        product = jnp.dot(table, windows, preferred_element_type=jnp.float32)
        mixed = jnp.where(lane_group == group, product, mixed)
    half_rows = tokens // halves
    for block in range(blocks):
        start = block * taps
        query = q_ref[start : start + taps, :].astype(jnp.float32)
        columns = slice(block * lanes, (block + 1) * lanes)
        half, row = start // half_rows, start % half_rows
        out_ref[half, 0, row : row + taps, :] = (query * mixed[:taps, columns]).astype(jnp.bfloat16)
        out_ref[half, 1, row : row + taps, :] = (
            query * mixed[taps:, columns] * keep_ref[...]
        ).astype(jnp.bfloat16)


def flipped(position, bits):
    result = position
    step = 1
    while step <= bits:
        if bits & step:
            result = result + step - 2 * step * ((position // step) % 2)
        step *= 2
    return result


def grad_kernel(
    seq_count,
    chan_count,
    own_ref,
    teacher_hbm,
    student_hbm,
    weight_ref,
    grad_ref,
    mixes,
    teacher_w,
    student_w,
    part,
    adjoint,
    transposed,
    *rest,
):
    bits = chan_count.bit_length() - 1
    received = rest[:bits]
    local_sem, seq_send, seq_recv, down_send, down_recv, up_send, up_recv = rest[bits:]
    seq_me = lax.axis_index("seq")
    chan_me = lax.axis_index("chan")
    units = seq_count * halves
    rows = part.shape[1]
    columns = part.shape[2]
    channels = mixes.shape[3]
    tile = min(512, columns)

    local = [
        pltpu.make_async_copy(own_ref, mixes.at[pl.ds(0, halves)], local_sem.at[0]),
        pltpu.make_async_copy(teacher_hbm, teacher_w, local_sem.at[1]),
        pltpu.make_async_copy(student_hbm, student_w, local_sem.at[2]),
    ]
    for copy in local:
        copy.start()

    chan_partners = [{"seq": seq_me, "chan": flipped(chan_me, 1 << bit)} for bit in range(bits)]
    seq_partners = [{"seq": flipped(seq_me, k), "chan": chan_me} for k in range(1, seq_count)]
    barrier = pltpu.get_barrier_semaphore()
    for partner in chan_partners + seq_partners:
        pl.semaphore_signal(
            barrier, inc=1, device_id=partner, device_id_type=pl.DeviceIdType.MESH
        )
    pl.semaphore_wait(barrier, len(chan_partners) + len(seq_partners))

    def seq_copy(unit, half, partner):
        return pltpu.make_async_remote_copy(
            src_ref=mixes.at[half],
            dst_ref=mixes.at[unit],
            send_sem=seq_send.at[unit],
            recv_sem=seq_recv.at[unit],
            device_id=partner,
            device_id_type=pl.DeviceIdType.MESH,
        )

    local[0].wait()
    for k in range(1, seq_count):
        for half in range(halves):
            seq_copy(k * halves + half, half, seq_partners[k - 1]).start()
    grad_ref[...] = jnp.zeros_like(grad_ref)
    local[1].wait()
    local[2].wait()

    side = [(chan_me // (1 << bit)) % 2 for bit in range(bits)]
    held = [0]
    for bit in range(bits):
        held.append(held[bit] + side[bit] * (rows >> (bit + 1)))

    def slab(offset, size):
        return pl.ds(pl.multiple_of(offset, 16), size)

    def down_copy(bit, unit):
        size = rows >> (bit + 1)
        away = held[bit] + (1 - side[bit]) * size
        return pltpu.make_async_remote_copy(
            src_ref=part.at[unit, slab(away, size)],
            dst_ref=received[bit].at[unit],
            send_sem=down_send.at[bit, unit],
            recv_sem=down_recv.at[bit, unit],
            device_id=chan_partners[bit],
            device_id_type=pl.DeviceIdType.MESH,
        )

    def up_copy(bit, unit, incoming=False):
        size = rows >> (bit + 1)
        start = held[bit] + (1 - side[bit]) * size if incoming else held[bit + 1]
        place = adjoint.at[unit, slab(start, size)]
        return pltpu.make_async_remote_copy(
            src_ref=place,
            dst_ref=place,
            send_sem=up_send.at[bit, unit],
            recv_sem=up_recv.at[bit, unit],
            device_id=chan_partners[bit],
            device_id_type=pl.DeviceIdType.MESH,
        )

    def multiply(unit):
        @pl.when(unit >= halves)
        def _():
            seq_copy(unit, 0, seq_partners[0]).wait_recv()

        @pl.loop(0, columns // tile)
        def _(step):
            span = pl.ds(pl.multiple_of(step * tile, tile), tile)
            student = jnp.dot(
                mixes[unit, 1], student_w[:, span], preferred_element_type=jnp.float32
            )
            teacher = jnp.dot(
                mixes[unit, 0], teacher_w[:, span], preferred_element_type=jnp.float32
            )
            part[unit, :, span] = (student - teacher).astype(jnp.bfloat16)

        down_copy(0, unit).start()

    def fold(bit, unit):
        size = rows >> (bit + 1)
        down_copy(bit, unit).wait_recv()
        kept = slab(held[bit + 1], size)
        total = part[unit, kept].astype(jnp.float32) + received[bit][unit].astype(jnp.float32)
        if bit + 1 < bits:
            part[unit, kept] = total.astype(jnp.bfloat16)
            down_copy(bit + 1, unit).start()
        else:
            residual = total.astype(jnp.bfloat16).astype(jnp.float32)
            adjoint[unit, kept] = (residual * weight_ref[unit][:, 0:1]).astype(jnp.bfloat16)
            up_copy(bit, unit).start()

    def spread(bit, unit):
        up_copy(bit, unit, True).wait_recv()
        up_copy(bit - 1, unit).start()

    def accumulate(unit):
        up_copy(0, unit, True).wait_recv()
        transposed[...] = mixes[unit, 1].T

        @pl.loop(0, columns // tile)
        def _(step):
            span = pl.ds(pl.multiple_of(step * tile, tile), tile)
            grad_ref[:, span] += jnp.dot(
                transposed[...], adjoint[unit, :, span], preferred_element_type=jnp.float32
            )

    stages = [multiply]
    stages += [functools.partial(fold, bit) for bit in range(bits)]
    stages += [functools.partial(spread, bit) for bit in range(bits - 1, 0, -1)]
    stages += [accumulate]
    last = len(stages) - 1
    order = list(range(last - 1, -1, -1)) + [last]

    @pl.loop(0, units + last)
    def _(step):
        for place in order:
            unit = step - place

            @pl.when(jnp.logical_and(unit >= 0, unit < units))
            def _():
                stages[place](unit)

    for k in range(1, seq_count):
        for half in range(halves):
            seq_copy(k * halves + half, half, seq_partners[k - 1]).wait_send()

    @pl.loop(0, units)
    def _(unit):
        for bit in range(bits):
            down_copy(bit, unit).wait_send()
            up_copy(bit, unit).wait_send()


def body(
    query_stream,
    key_stream,
    value_stream,
    teacher_filter,
    student_filter,
    group_mask,
    base_ids,
    teacher_proj,
    student_proj,
):
    tok_rows, channels = query_stream.shape
    groups, taps = teacher_filter.shape
    width = channels // groups
    seq_count = lax.axis_size("seq")
    chan_count = lax.axis_size("chan")
    columns = teacher_proj.shape[1]
    scale = float(tok_rows * seq_count) ** (-0.5)

    tail = (
        key_stream[tok_rows - taps :].astype(jnp.float32)
        * value_stream[tok_rows - taps :].astype(jnp.float32)
    ).astype(jnp.bfloat16)
    prior = shifted(tail, "seq", 1)
    filters = jnp.stack([teacher_filter, student_filter])
    base_rows = jnp.concatenate(
        [
            jnp.zeros((2, groups, 1), jnp.float32),
            filters[:, :, ::-1],
            jnp.zeros((2, groups, taps - 1), jnp.float32),
        ],
        axis=2,
    )
    keep = jnp.broadcast_to(group_mask.astype(jnp.float32)[:, None], (groups, width))
    keep = keep.reshape(1, channels)
    unit_rows = tok_rows // halves
    stream_spec = pl.BlockSpec((tok_rows, lanes), lambda i: (0, i))
    mixes = pl.pallas_call(
        functools.partial(mix_kernel, taps, width),
        grid=(channels // lanes,),
        out_shape=jax.ShapeDtypeStruct((halves, 2, unit_rows, channels), jnp.bfloat16),
        in_specs=[
            stream_spec,
            stream_spec,
            stream_spec,
            pl.BlockSpec((taps, lanes), lambda i: (0, i)),
            pl.BlockSpec((2, lanes // width, 2 * taps), lambda i: (0, i, 0)),
            pl.BlockSpec((1, lanes), lambda i: (0, i)),
        ],
        out_specs=pl.BlockSpec((halves, 2, unit_rows, lanes), lambda i: (0, 0, 0, i)),
        scratch_shapes=[pltpu.VMEM((2 * taps, tok_rows // taps * lanes), jnp.bfloat16)],
        name="mix",
    )(query_stream, key_stream, value_stream, prior, base_rows, keep)

    bits = chan_count.bit_length() - 1
    units = seq_count * halves
    piece = unit_rows // chan_count
    seq_me = lax.axis_index("seq")
    chan_me = lax.axis_index("chan")
    offset = sum(((chan_me // (1 << bit)) % 2) * (unit_rows >> (bit + 1)) for bit in range(bits))
    weights = jnp.where(base_ids >= 4, repeat_weight, 1.0).astype(jnp.float32) * scale
    here = jnp.stack(
        [
            lax.dynamic_slice_in_dim(
                weights, flipped(seq_me, u // halves) * tok_rows + (u % halves) * unit_rows + offset, piece
            )
            for u in range(units)
        ]
    )
    here = jnp.broadcast_to(here[:, :, None], (units, piece, lanes))

    any_spec = pl.BlockSpec(memory_space=pl.ANY)
    vmem_spec = pl.BlockSpec(memory_space=pltpu.VMEM)
    dma = pltpu.SemaphoreType.DMA
    return pl.pallas_call(
        functools.partial(grad_kernel, seq_count, chan_count),
        out_shape=jax.ShapeDtypeStruct((channels, columns), jnp.float32),
        in_specs=[any_spec, any_spec, any_spec, vmem_spec],
        out_specs=vmem_spec,
        scratch_shapes=[
            pltpu.VMEM((units, 2, unit_rows, channels), jnp.bfloat16),
            pltpu.VMEM(teacher_proj.shape, jnp.bfloat16),
            pltpu.VMEM(student_proj.shape, jnp.bfloat16),
            pltpu.VMEM((units, unit_rows, columns), jnp.bfloat16),
            pltpu.VMEM((units, unit_rows, columns), jnp.bfloat16),
            pltpu.VMEM((channels, unit_rows), jnp.bfloat16),
            *[
                pltpu.VMEM((units, unit_rows >> (bit + 1), columns), jnp.bfloat16)
                for bit in range(bits)
            ],
            dma((3,)),
            dma((units,)),
            dma((units,)),
            dma((bits, units)),
            dma((bits, units)),
            dma((bits, units)),
            dma((bits, units)),
        ],
        compiler_params=pltpu.CompilerParams(
            collective_id=0, has_side_effects=True, vmem_limit_bytes=vmem_limit
        ),
        name="grad",
    )(mixes, teacher_proj, student_proj, here)


def solution(mesh):
    placed = (
        P("seq", "chan"),
        P("seq", "chan"),
        P("seq", "chan"),
        P("chan", None),
        P("chan", None),
        P("chan"),
        P(),
        P("chan", "seq"),
        P("chan", "seq"),
    )
    return jax.shard_map(
        body, mesh=mesh, in_specs=placed, out_specs=P("chan", "seq"), check_vma=False
    )
```

profile of v0, /device:TPU:7, one launch (start us, length us, event | category | flops | bytes accessed | tf_op | source)
XLA Modules:
  0.0 207.3 jit_solution(14415205568585896529)
XLA Ops:
  0.0 1.1 multiply_convert_fusion
  1.1 1.3 collective-permute-start
  2.5 0.7 select_multiply_fusion
  3.2 0.8 pad_maximum_fusion
  4.0 0.1 dynamic-slice_bitcast_fusion
  4.1 0.7 convert_element_type.15
  4.8 0.1 pad.2.clone
  4.9 0.1 broadcast_in_dim.28
  4.9 0.7 reshape.5.keep_ref
  5.6 0.1 rev.3
  5.7 0.8 maximum_maximum_fusion.rows_ref
  6.5 3.7 %collective-permute-done.prior_ref = bf16[128,1024]{1,0:T(8,128)(2,1)S(1)} collective-permute-done((bf16[128,1024]{1,0:T(8,128)(2,1)S(1)}, bf16[128,1024]{1,0:T(8,128)(2,1)S(1)}, u32[]{:S(2)}, u32[]{:S(2)}) %collective-permute-start) | collective-permute-done | bytes 262176 | tf_op jit(solution)/shard_map/ppermute | solution.py:19
  10.2 0.0 copy-start
  10.2 0.7 copy-done
  10.9 9.4 %mix.1.own_ref = bf16[2,2,256,1024]{3,2,1,0:T(8,128)(2,1)} custom-call(bf16[512,1024]{1,0:T(8,128)(2,1)} %q_ref.1, bf16[512,1024]{1,0:T(8,128)(2,1)} %k_ref.1, bf16[512,1024]{1,0:T(8,128)(2,1)} %v_ref.1, bf16[128,1024]{1,0:T(8,128)(2,1)} %copy-done, f32[2,64,256]{2,1,0:T(8,128)} %maximum_maximum_fusion.rows_ref, f32[1,1024]{1,0:T(1,128)} %reshape.5.keep_ref), custom_call_target="tpu_custom_call" | custom-call | tf_op jit(solution)/shard_map/mix/pallas_call | solution.py:271
  20.3 0.8 broadcast_in_dim.31.weight_ref
  21.0 178.4 %grad.1 = f32[1024,2048]{1,0:T(8,128)} custom-call(bf16[2,2,256,1024]{3,2,1,0:T(8,128)(2,1)} %mix.1.own_ref, bf16[1024,2048]{1,0:T(8,128)(2,1)} %teacher_hbm.1, bf16[1024,2048]{1,0:T(8,128)(2,1)} %student_hbm.1, f32[8,32,128]{2,1,0:T(8,128)} %broadcast_in_dim.31.weight_ref), custom_call_target="tpu_custom_call" | custom-call | tf_op jit(solution)/shard_map/grad/pallas_call | solution.py:308
  199.5 7.9 %copy.11 = f32[1024,2048]{1,0:T(8,128)} copy(f32[1024,2048]{1,0:T(8,128)} %grad.1) | data formatting | bytes 16777216
  (3 shorter events, 0.0 us)
Async XLA Ops:
  1.1 9.1 %collective-permute-start = (bf16[128,1024]{1,0:T(8,128)(2,1)S(1)}, bf16[128,1024]{1,0:T(8,128)(2,1)S(1)}, u32[]{:S(2)}, u32[]{:S(2)}) collective-permute-start(bf16[128,1024]{1,0:T(8,128)(2,1)S(1)} %multiply_convert_fusion), channel_id=1, source_target_pairs={{0,8},{8,16},{16,24},{1,9},{9,17},{17,25},{2,10},{10,18},{18,26},{... | collective-permute-start | bytes 786440 | tf_op jit(solution)/shard_map/ppermute | solution.py:19
  10.2 0.7 copy-start
where the time goes:
time: 209 us; the launch traced here: 207 us
  Pallas kernels  188 us (90%)
  local copies, waits for them, and re-layouts  10.4 us (5%)
  other arithmetic  4.01 us (2%)
  waiting for transfers between devices  3.69 us (2%)
    pallas_call x1, Pallas kernels, body(): pl.pallas_call(functools.partial(grad_kernel, seq_count, chan_count), out...  178 us
    pallas_call x1, Pallas kernels, body(): pl.pallas_call(functools.partial(mix_kernel, taps, width), grid=(channels...  9.41 us
    unnamed x3, local copies, waits for them, and re-layouts  8.57 us
  transfers between devices with their start and end apart: 1, of which 1 were waited for; matrix products, arithmetic and copies ran while one was open for 2% of the time, Pallas kernels for 0%

commit v1 on v0

v1 whole, which is shorter than its diff:
```python
import functools

import jax
import jax.numpy as jnp
from jax import lax
from jax.experimental import pallas as pl
from jax.experimental.pallas import tpu as pltpu
from jax.sharding import PartitionSpec as P

repeat_weight = 0.1
lanes = 128
halves = 2
cuts = 2
vmem_limit = 66_000_000


def shifted(value, axis, steps):
    count = lax.axis_size(axis)
    initial, last = (max(0, -steps), min(count, count - steps))
    return lax.ppermute(value, axis, [(source, source + steps) for source in range(initial, last)])


def mix_kernel(taps, width, q_ref, k_ref, v_ref, prior_ref, rows_ref, keep_ref, out_ref, ext_ref):
    tokens = q_ref.shape[0]
    blocks = tokens // taps
    group_count = lanes // width
    gated = (k_ref[...].astype(jnp.float32) * v_ref[...].astype(jnp.float32)).astype(jnp.bfloat16)
    ext_ref[0:taps, 0:lanes] = prior_ref[...]
    for block in range(blocks):
        piece = gated[block * taps : (block + 1) * taps]
        ext_ref[taps : 2 * taps, block * lanes : (block + 1) * lanes] = piece
        if block + 1 < blocks:
            ext_ref[0:taps, (block + 1) * lanes : (block + 2) * lanes] = piece
    windows = ext_ref[...]
    lane_group = lax.broadcasted_iota(jnp.int32, (2 * taps, blocks * lanes), 1) % lanes // width
    mixed = jnp.zeros((2 * taps, blocks * lanes), jnp.float32)
    for group in range(group_count):
        tables = []
        for kind in range(2):
            base = jnp.broadcast_to(rows_ref[kind, group : group + 1, :], (taps, 2 * taps))
            tables.append(pltpu.roll(base, 0, 1, stride=1, stride_axis=0))
        table = jnp.concatenate(tables, axis=0).astype(jnp.bfloat16)
        product = jnp.dot(table, windows, preferred_element_type=jnp.float32)
        mixed = jnp.where(lane_group == group, product, mixed)
    half_rows = tokens // halves
    for block in range(blocks):
        start = block * taps
        query = q_ref[start : start + taps, :].astype(jnp.float32)
        columns = slice(block * lanes, (block + 1) * lanes)
        half, row = start // half_rows, start % half_rows
        out_ref[half, 0, row : row + taps, :] = (query * mixed[:taps, columns]).astype(jnp.bfloat16)
        out_ref[half, 1, row : row + taps, :] = (
            query * mixed[taps:, columns] * keep_ref[...]
        ).astype(jnp.bfloat16)


def flipped(position, bits):
    result = position
    step = 1
    while step <= bits:
        if bits & step:
            result = result + step - 2 * step * ((position // step) % 2)
        step *= 2
    return result


def unit_order(seq_count):
    near = [k for k in (1, 2) if k < seq_count]
    order = [(0, half) for half in range(halves)]
    order += [(k, half) for half in range(halves) for k in near]
    return order + [(k, half) for k in range(3, seq_count) for half in range(halves)]


def chan_bit(position, bit):
    return (position // (1 << bit)) % 2


def middle_steps(chan_count):
    bits = chan_count.bit_length() - 1
    assert bits >= 3 and chan_count == 1 << bits
    return [(6, 2)] + [(1 << bit, bit) for bit in range(3, bits)]


def grad_kernel(
    seq_count,
    chan_count,
    own_ref,
    teacher_hbm,
    student_hbm,
    weight_ref,
    grad_ref,
    mixes,
    teacher_w,
    student_w,
    part,
    adjoint,
    transposed,
    total_ref,
    pair_in,
    edge_in,
    *rest,
):
    steps = middle_steps(chan_count)
    count = len(steps)
    middle_in = rest[:count]
    (
        local_sem,
        seq_send,
        seq_recv,
        pair_send,
        pair_recv,
        edge_send,
        edge_recv,
        down_send,
        down_recv,
        up_send,
        up_recv,
    ) = rest[count:]
    seq_me = lax.axis_index("seq")
    chan_me = lax.axis_index("chan")
    order = unit_order(seq_count)
    items = len(order) * cuts
    rows = part.shape[1]
    columns = part.shape[2]
    tile = min(512, columns)

    local = [
        pltpu.make_async_copy(own_ref, mixes.at[pl.ds(0, halves)], local_sem.at[0]),
        pltpu.make_async_copy(teacher_hbm, teacher_w, local_sem.at[1]),
        pltpu.make_async_copy(student_hbm, student_w, local_sem.at[2]),
    ]
    for copy in local:
        copy.start()

    def along_chan(flips):
        return {"seq": seq_me, "chan": flipped(chan_me, flips)}

    pair_partner = along_chan(1)
    edge_partner = along_chan(2)
    middle_partners = [along_chan(flips) for flips, _ in steps]
    seq_partners = [{"seq": flipped(seq_me, k), "chan": chan_me} for k in range(1, seq_count)]
    everyone = [pair_partner, edge_partner] + middle_partners + seq_partners
    barrier = pltpu.get_barrier_semaphore()
    for partner in everyone:
        pl.semaphore_signal(
            barrier, inc=1, device_id=partner, device_id_type=pl.DeviceIdType.MESH
        )
    pl.semaphore_wait(barrier, len(everyone))

    def remote(source, target, send_sem, recv_sem, partner):
        return pltpu.make_async_remote_copy(
            src_ref=source,
            dst_ref=target,
            send_sem=send_sem,
            recv_sem=recv_sem,
            device_id=partner,
            device_id_type=pl.DeviceIdType.MESH,
        )

    def seq_copy(unit, half, partner):
        return remote(
            mixes.at[half], mixes.at[unit], seq_send.at[unit], seq_recv.at[unit], partner
        )

    local[0].wait()
    for unit in range(halves, len(order)):
        k, half = order[unit]
        seq_copy(unit, half, seq_partners[k - 1]).start()
    total_ref[...] = jnp.zeros_like(total_ref)
    local[1].wait()
    local[2].wait()

    half_size = rows // 2
    core = chan_bit(chan_me, 0)
    inner = chan_bit(chan_me, 1) != chan_bit(chan_me, 2)
    mine = core * half_size
    others = (1 - core) * half_size
    held = [mine]
    away = []
    for index, (_, bit) in enumerate(steps):
        size = half_size >> (index + 1)
        side = chan_bit(chan_me, bit)
        away.append(held[index] + (1 - side) * size)
        held.append(held[index] + side * size)

    def slab(offset, size):
        return pl.ds(pl.multiple_of(offset, 16), size)

    def pair_down(item):
        source = part.at[item, slab(others, half_size)]
        return remote(
            source, pair_in.at[item], pair_send.at[0, item], pair_recv.at[0, item], pair_partner
        )

    def pair_up(item, incoming=False):
        place = adjoint.at[item, slab(others if incoming else mine, half_size)]
        return remote(place, place, pair_send.at[1, item], pair_recv.at[1, item], pair_partner)

    def edge_down(item):
        source = part.at[item, slab(mine, half_size)]
        return remote(
            source, edge_in.at[item], edge_send.at[0, item], edge_recv.at[0, item], edge_partner
        )

    def edge_up(item):
        place = adjoint.at[item, slab(mine, half_size)]
        return remote(place, place, edge_send.at[1, item], edge_recv.at[1, item], edge_partner)

    def middle_down(index, item):
        source = part.at[item, slab(away[index], half_size >> (index + 1))]
        return remote(
            source,
            middle_in[index].at[item],
            down_send.at[index, item],
            down_recv.at[index, item],
            middle_partners[index],
        )

    def middle_up(index, item, incoming=False):
        start = away[index] if incoming else held[index + 1]
        place = adjoint.at[item, slab(start, half_size >> (index + 1))]
        return remote(
            place,
            place,
            up_send.at[index, item],
            up_recv.at[index, item],
            middle_partners[index],
        )

    def multiply(item):
        unit = item // cuts
        first = item % cuts * columns

        @pl.when(jnp.logical_and(unit >= halves, item % cuts == 0))
        def _():
            seq_copy(unit, 0, seq_partners[0]).wait_recv()

        @pl.loop(0, columns // tile)
        def _(step):
            span = pl.ds(pl.multiple_of(step * tile, tile), tile)
            source = pl.ds(pl.multiple_of(first + step * tile, tile), tile)
            student = jnp.dot(
                mixes[unit, 1], student_w[:, source], preferred_element_type=jnp.float32
            )
            teacher = jnp.dot(
                mixes[unit, 0], teacher_w[:, source], preferred_element_type=jnp.float32
            )
            part[item, :, span] = (student - teacher).astype(jnp.bfloat16)

        pair_down(item).start()

    def added(item, offset, size, arrived):
        kept = part[item, slab(offset, size)].astype(jnp.float32)
        return kept + arrived[item].astype(jnp.float32)

    def fold_pair(item):
        pair_down(item).wait_recv()
        part[item, slab(mine, half_size)] = added(item, mine, half_size, pair_in).astype(
            jnp.bfloat16
        )

        @pl.when(jnp.logical_not(inner))
        def _():
            edge_down(item).start()

    def fold_edge(item):
        @pl.when(inner)
        def _():
            edge_down(item).wait_recv()
            part[item, slab(mine, half_size)] = added(item, mine, half_size, edge_in).astype(
                jnp.bfloat16
            )
            middle_down(0, item).start()

    def fold_middle(index, item):
        @pl.when(inner)
        def _():
            middle_down(index, item).wait_recv()
            size = half_size >> (index + 1)
            start = held[index + 1]
            total = added(item, start, size, middle_in[index])
            if index + 1 < count:
                part[item, slab(start, size)] = total.astype(jnp.bfloat16)
                middle_down(index + 1, item).start()
            else:
                residual = total.astype(jnp.bfloat16).astype(jnp.float32)
                adjoint[item, slab(start, size)] = (
                    residual * weight_ref[item // cuts][:, 0:1]
                ).astype(jnp.bfloat16)
                middle_up(index, item).start()

    def spread_middle(index, item):
        @pl.when(inner)
        def _():
            middle_up(index, item, True).wait_recv()
            if index > 0:
                middle_up(index - 1, item).start()
            else:
                edge_up(item).start()
                pair_up(item).start()

    def spread_edge(item):
        @pl.when(jnp.logical_not(inner))
        def _():
            edge_up(item).wait_recv()
            pair_up(item).start()

    def accumulate(item):
        unit = item // cuts
        first = item % cuts * columns
        pair_up(item, True).wait_recv()

        @pl.when(item % cuts == 0)
        def _():
            transposed[...] = mixes[unit, 1].T

        @pl.loop(0, columns // tile)
        def _(step):
            span = pl.ds(pl.multiple_of(step * tile, tile), tile)
            target = pl.ds(pl.multiple_of(first + step * tile, tile), tile)
            total_ref[:, target] += jnp.dot(
                transposed[...], adjoint[item, :, span], preferred_element_type=jnp.float32
            )

    stages = [multiply, fold_pair, fold_edge]
    stages += [functools.partial(fold_middle, index) for index in range(count)]
    stages += [functools.partial(spread_middle, index) for index in range(count - 1, -1, -1)]
    stages += [spread_edge, accumulate]
    last = len(stages) - 1
    places = list(range(last - 1, -1, -1)) + [last]

    @pl.loop(0, items + last)
    def _(step):
        for place in places:
            item = step - place

            @pl.when(jnp.logical_and(item >= 0, item < items))
            def _():
                stages[place](item)

    grad_ref[...] = total_ref[...].astype(grad_ref.dtype)

    for unit in range(halves, len(order)):
        k, half = order[unit]
        seq_copy(unit, half, seq_partners[k - 1]).wait_send()

    @pl.loop(0, items)
    def _(item):
        pair_down(item).wait_send()
        pair_up(item).wait_send()

        @pl.when(inner)
        def _():
            edge_up(item).wait_send()
            for index in range(count):
                middle_down(index, item).wait_send()
                middle_up(index, item).wait_send()

        @pl.when(jnp.logical_not(inner))
        def _():
            edge_down(item).wait_send()


def body(
    query_stream,
    key_stream,
    value_stream,
    teacher_filter,
    student_filter,
    group_mask,
    base_ids,
    teacher_proj,
    student_proj,
):
    tok_rows, channels = query_stream.shape
    groups, taps = teacher_filter.shape
    width = channels // groups
    seq_count = lax.axis_size("seq")
    chan_count = lax.axis_size("chan")
    columns = teacher_proj.shape[1]
    scale = float(tok_rows * seq_count) ** (-0.5)

    tail = (
        key_stream[tok_rows - taps :].astype(jnp.float32)
        * value_stream[tok_rows - taps :].astype(jnp.float32)
    ).astype(jnp.bfloat16)
    prior = shifted(tail, "seq", 1)
    filters = jnp.stack([teacher_filter, student_filter])
    base_rows = jnp.concatenate(
        [
            jnp.zeros((2, groups, 1), jnp.float32),
            filters[:, :, ::-1],
            jnp.zeros((2, groups, taps - 1), jnp.float32),
        ],
        axis=2,
    )
    keep = jnp.broadcast_to(group_mask.astype(jnp.float32)[:, None], (groups, width))
    keep = keep.reshape(1, channels)
    unit_rows = tok_rows // halves
    stream_spec = pl.BlockSpec((tok_rows, lanes), lambda i: (0, i))
    mixes = pl.pallas_call(
        functools.partial(mix_kernel, taps, width),
        grid=(channels // lanes,),
        out_shape=jax.ShapeDtypeStruct((halves, 2, unit_rows, channels), jnp.bfloat16),
        in_specs=[
            stream_spec,
            stream_spec,
            stream_spec,
            pl.BlockSpec((taps, lanes), lambda i: (0, i)),
            pl.BlockSpec((2, lanes // width, 2 * taps), lambda i: (0, i, 0)),
            pl.BlockSpec((1, lanes), lambda i: (0, i)),
        ],
        out_specs=pl.BlockSpec((halves, 2, unit_rows, lanes), lambda i: (0, 0, 0, i)),
        scratch_shapes=[pltpu.VMEM((2 * taps, tok_rows // taps * lanes), jnp.bfloat16)],
        name="mix",
    )(query_stream, key_stream, value_stream, prior, base_rows, keep)

    order = unit_order(seq_count)
    units = len(order)
    items = units * cuts
    steps = middle_steps(chan_count)
    half_size = unit_rows // 2
    piece = half_size >> len(steps)
    seq_me = lax.axis_index("seq")
    chan_me = lax.axis_index("chan")
    offset = chan_bit(chan_me, 0) * half_size + sum(
        chan_bit(chan_me, bit) * (half_size >> (index + 1)) for index, (_, bit) in enumerate(steps)
    )
    weights = jnp.where(base_ids >= 4, repeat_weight, 1.0).astype(jnp.float32) * scale
    here = jnp.stack(
        [
            lax.dynamic_slice_in_dim(
                weights, flipped(seq_me, k) * tok_rows + half * unit_rows + offset, piece
            )
            for k, half in order
        ]
    )
    here = jnp.broadcast_to(here[:, :, None], (units, piece, lanes))

    any_spec = pl.BlockSpec(memory_space=pl.ANY)
    vmem_spec = pl.BlockSpec(memory_space=pltpu.VMEM)
    dma = pltpu.SemaphoreType.DMA
    cut = columns // cuts
    result = pl.pallas_call(
        functools.partial(grad_kernel, seq_count, chan_count),
        out_shape=jax.ShapeDtypeStruct((channels, columns), jnp.bfloat16),
        in_specs=[any_spec, any_spec, any_spec, vmem_spec],
        out_specs=vmem_spec,
        scratch_shapes=[
            pltpu.VMEM((units, 2, unit_rows, channels), jnp.bfloat16),
            pltpu.VMEM(teacher_proj.shape, jnp.bfloat16),
            pltpu.VMEM(student_proj.shape, jnp.bfloat16),
            pltpu.VMEM((items, unit_rows, cut), jnp.bfloat16),
            pltpu.VMEM((items, unit_rows, cut), jnp.bfloat16),
            pltpu.VMEM((channels, unit_rows), jnp.bfloat16),
            pltpu.VMEM((channels, columns), jnp.float32),
            pltpu.VMEM((items, half_size, cut), jnp.bfloat16),
            pltpu.VMEM((items, half_size, cut), jnp.bfloat16),
            *[
                pltpu.VMEM((items, half_size >> (index + 1), cut), jnp.bfloat16)
                for index in range(len(steps))
            ],
            dma((3,)),
            dma((units,)),
            dma((units,)),
            dma((2, items)),
            dma((2, items)),
            dma((2, items)),
            dma((2, items)),
            dma((len(steps), items)),
            dma((len(steps), items)),
            dma((len(steps), items)),
            dma((len(steps), items)),
        ],
        compiler_params=pltpu.CompilerParams(
            collective_id=0, has_side_effects=True, vmem_limit_bytes=vmem_limit
        ),
        name="grad",
    )(mixes, teacher_proj, student_proj, here)
    return result.astype(jnp.float32)


def solution(mesh):
    placed = (
        P("seq", "chan"),
        P("seq", "chan"),
        P("seq", "chan"),
        P("chan", None),
        P("chan", None),
        P("chan"),
        P(),
        P("chan", "seq"),
        P("chan", "seq"),
    )
    return jax.shard_map(
        body, mesh=mesh, in_specs=placed, out_specs=P("chan", "seq"), check_vma=False
    )
```

time: 209 us -> 188 us (0.90)
  Pallas kernels: 188 us -> 169 us
  local copies, waits for them, and re-layouts: 10.4 us -> 2.55 us
  other arithmetic: 4.01 us -> 10.7 us
    pallas_call x1, Pallas kernels: 178 us -> 159 us  [body(): pl.pallas_call(functools.partial(grad_kernel, seq_count, chan_count), out...]
    unnamed x3 -> x2, local copies, waits for them, and re-layouts: 8.57 us -> 0.69 us
    convert_element_type x0 -> x1, other arithmetic: none -> 6.66 us  [body(): return result.astype(jnp.float32)]
where the time goes in v1:
time: 188 us; the launch traced here: 187 us
  Pallas kernels  169 us (90%)
  other arithmetic  10.7 us (6%)
  waiting for transfers between devices  3.71 us (2%)
  local copies, waits for them, and re-layouts  2.55 us (1%)
    pallas_call x1, Pallas kernels, body(): pl.pallas_call(functools.partial(grad_kernel, seq_count, chan_count), out...  159 us
    pallas_call x1, Pallas kernels, body(): pl.pallas_call(functools.partial(mix_kernel, taps, width), grid=(channels...  9.41 us
    convert_element_type x1, other arithmetic, body(): return result.astype(jnp.float32)  6.66 us
  transfers between devices with their start and end apart: 1, of which 1 were waited for; matrix products, arithmetic and copies ran while one was open for 2% of the time, Pallas kernels for 0%

profile of v1, /device:TPU:7, one launch (start us, length us, event | category | flops | bytes accessed | tf_op | source)
XLA Modules:
  0.0 187.2 jit_solution(13013691578284241210)
XLA Ops:
  0.0 1.1 multiply_convert_fusion
  1.1 1.3 collective-permute-start
  2.5 0.7 select_multiply_fusion
  3.2 0.8 pad_maximum_fusion
  4.0 0.1 dynamic-slice_bitcast_fusion
  4.1 0.7 convert_element_type.18
  4.7 0.1 pad.2.clone
  4.8 0.1 broadcast_in_dim.28
  4.9 0.7 reshape.5.keep_ref
  5.6 0.1 rev.3
  5.7 0.8 maximum_maximum_fusion.rows_ref
  6.5 3.7 %collective-permute-done.prior_ref = bf16[128,1024]{1,0:T(8,128)(2,1)S(1)} collective-permute-done((bf16[128,1024]{1,0:T(8,128)(2,1)S(1)}, bf16[128,1024]{1,0:T(8,128)(2,1)S(1)}, u32[]{:S(2)}, u32[]{:S(2)}) %collective-permute-start) | collective-permute-done | bytes 262176 | tf_op jit(solution)/shard_map/ppermute | solution.py:20
  10.2 0.0 copy-start
  10.2 0.7 copy-done
  10.9 9.4 %mix.1.own_ref = bf16[2,2,256,1024]{3,2,1,0:T(8,128)(2,1)} custom-call(bf16[512,1024]{1,0:T(8,128)(2,1)} %q_ref.1, bf16[512,1024]{1,0:T(8,128)(2,1)} %k_ref.1, bf16[512,1024]{1,0:T(8,128)(2,1)} %v_ref.1, bf16[128,1024]{1,0:T(8,128)(2,1)} %copy-done, f32[2,64,256]{2,1,0:T(8,128)} %maximum_maximum_fusion.rows_ref, f32[1,1024]{1,0:T(1,128)} %reshape.5.keep_ref), custom_call_target="tpu_custom_call" | custom-call | tf_op jit(solution)/shard_map/mix/pallas_call | solution.py:401
  20.3 0.8 broadcast_in_dim.31.weight_ref
  21.1 159.5 %grad.1 = bf16[1024,2048]{1,0:T(8,128)(2,1)} custom-call(bf16[2,2,256,1024]{3,2,1,0:T(8,128)(2,1)} %mix.1.own_ref, bf16[1024,2048]{1,0:T(8,128)(2,1)} %teacher_hbm.1, bf16[1024,2048]{1,0:T(8,128)(2,1)} %student_hbm.1, f32[8,64,128]{2,1,0:T(8,128)} %broadcast_in_dim.31.weight_ref), custom_call_target="tpu_custom_call" | custom-call | tf_op jit(solution)/shard_map/grad/pallas_call | solution.py:444
  180.6 6.7 %convert_element_type.19 = f32[1024,2048]{1,0:T(8,128)} convert(bf16[1024,2048]{1,0:T(8,128)(2,1)} %grad.1) | non-fusion elementwise | flops 2097152 | bytes 12582912 | tf_op jit(solution)/shard_map/convert_element_type | solution.py:480
  (3 shorter events, 0.0 us)
Async XLA Ops:
  1.1 9.1 %collective-permute-start = (bf16[128,1024]{1,0:T(8,128)(2,1)S(1)}, bf16[128,1024]{1,0:T(8,128)(2,1)S(1)}, u32[]{:S(2)}, u32[]{:S(2)}) collective-permute-start(bf16[128,1024]{1,0:T(8,128)(2,1)S(1)} %multiply_convert_fusion), channel_id=1, source_target_pairs={{0,8},{8,16},{16,24},{1,9},{9,17},{17,25},{2,10},{10,18},{18,26},{... | collective-permute-start | bytes 786440 | tf_op jit(solution)/shard_map/ppermute | solution.py:20
  10.2 0.7 copy-start

commit v2 on v1

--- a/solution.py
+++ b/solution.py
@@ -10,7 +10,8 @@
 repeat_weight = 0.1
 lanes = 128
 halves = 2
-cuts = 2
+cuts = 4
+lag = 2
 vmem_limit = 66_000_000
 
 
@@ -65,9 +66,8 @@
 
 
 def unit_order(seq_count):
-    near = [k for k in (1, 2) if k < seq_count]
-    order = [(0, half) for half in range(halves)]
-    order += [(k, half) for half in range(halves) for k in near]
+    assert seq_count >= 4
+    order = [(0, half) for half in range(halves)] + [(1, 0), (2, 1), (1, 1), (2, 0)]
     return order + [(k, half) for k in range(3, seq_count) for half in range(halves)]
 
 
@@ -165,7 +165,8 @@
     local[0].wait()
     for unit in range(halves, len(order)):
         k, half = order[unit]
-        seq_copy(unit, half, seq_partners[k - 1]).start()
+        if k != 3:
+            seq_copy(unit, half, seq_partners[k - 1]).start()
     total_ref[...] = jnp.zeros_like(total_ref)
     local[1].wait()
     local[2].wait()
@@ -234,6 +235,20 @@
         @pl.when(jnp.logical_and(unit >= halves, item % cuts == 0))
         def _():
             seq_copy(unit, 0, seq_partners[0]).wait_recv()
+
+        for near, half in ((1, 0), (2, 1)):
+            slot = order.index((near, half))
+            far = order.index((3, half))
+
+            @pl.when(item == slot * cuts)
+            def _():
+                remote(
+                    mixes.at[slot],
+                    mixes.at[far],
+                    seq_send.at[far],
+                    seq_recv.at[far],
+                    seq_partners[2 - near],
+                ).start()
 
         @pl.loop(0, columns // tile)
         def _(step):
@@ -329,10 +344,10 @@
     last = len(stages) - 1
     places = list(range(last - 1, -1, -1)) + [last]
 
-    @pl.loop(0, items + last)
+    @pl.loop(0, items + lag * last)
     def _(step):
         for place in places:
-            item = step - place
+            item = step - lag * place
 
             @pl.when(jnp.logical_and(item >= 0, item < items))
             def _():

time: 188 us -> 156 us (0.83)
  Pallas kernels: 169 us -> 136 us
    pallas_call x1, Pallas kernels: 159 us -> 127 us  [body(): pl.pallas_call(functools.partial(grad_kernel, seq_count, chan_count), out...]
  transfers between devices with their start and end apart: 1 -> 1, of which waited for: 1 -> 1; matrix products, arithmetic and copies ran while one was open for 2% -> 3% of each run, Pallas kernels for 0% -> 0%
where the time goes in v2:
time: 156 us; the launch traced here: 154 us
  Pallas kernels  136 us (87%)
  other arithmetic  10.7 us (7%)
  waiting for transfers between devices  3.71 us (2%)
  local copies, waits for them, and re-layouts  2.55 us (2%)
    pallas_call x1, Pallas kernels, body(): pl.pallas_call(functools.partial(grad_kernel, seq_count, chan_count), out...  127 us
    pallas_call x1, Pallas kernels, body(): pl.pallas_call(functools.partial(mix_kernel, taps, width), grid=(channels...  9.41 us
    convert_element_type x1, other arithmetic, body(): return result.astype(jnp.float32)  6.66 us
    ppermute x1, waiting for transfers between devices, shifted(): lax.ppermute(value, axis, [(source, source + steps) for source in range(i...  3.71 us
  transfers between devices with their start and end apart: 1, of which 1 were waited for; matrix products, arithmetic and copies ran while one was open for 3% of the time, Pallas kernels for 0%

profile of v2, /device:TPU:7, one launch (start us, length us, event | category | flops | bytes accessed | tf_op | source)
XLA Modules:
  0.0 154.3 jit_solution(12738907674327765235)
XLA Ops:
  0.0 1.1 multiply_convert_fusion
  1.1 1.3 collective-permute-start
  2.5 0.7 select_multiply_fusion
  3.2 0.8 pad_maximum_fusion
  4.0 0.1 dynamic-slice_bitcast_fusion
  4.1 0.7 convert_element_type.18
  4.7 0.1 pad.2.clone
  4.8 0.1 broadcast_in_dim.28
  4.9 0.7 reshape.5.keep_ref
  5.6 0.1 rev.3
  5.7 0.8 maximum_maximum_fusion.rows_ref
  6.5 3.7 %collective-permute-done.prior_ref = bf16[128,1024]{1,0:T(8,128)(2,1)S(1)} collective-permute-done((bf16[128,1024]{1,0:T(8,128)(2,1)S(1)}, bf16[128,1024]{1,0:T(8,128)(2,1)S(1)}, u32[]{:S(2)}, u32[]{:S(2)}) %collective-permute-start) | collective-permute-done | bytes 262176 | tf_op jit(solution)/shard_map/ppermute | solution.py:21
  10.2 0.0 copy-start
  10.2 0.7 copy-done
  10.9 9.4 %mix.1.own_ref = bf16[2,2,256,1024]{3,2,1,0:T(8,128)(2,1)} custom-call(bf16[512,1024]{1,0:T(8,128)(2,1)} %q_ref.1, bf16[512,1024]{1,0:T(8,128)(2,1)} %k_ref.1, bf16[512,1024]{1,0:T(8,128)(2,1)} %v_ref.1, bf16[128,1024]{1,0:T(8,128)(2,1)} %copy-done, f32[2,64,256]{2,1,0:T(8,128)} %maximum_maximum_fusion.rows_ref, f32[1,1024]{1,0:T(1,128)} %reshape.5.keep_ref), custom_call_target="tpu_custom_call" | custom-call | tf_op jit(solution)/shard_map/mix/pallas_call | solution.py:416
  20.3 0.8 broadcast_in_dim.31.weight_ref
  21.1 126.6 %grad.1 = bf16[1024,2048]{1,0:T(8,128)(2,1)} custom-call(bf16[2,2,256,1024]{3,2,1,0:T(8,128)(2,1)} %mix.1.own_ref, bf16[1024,2048]{1,0:T(8,128)(2,1)} %teacher_hbm.1, bf16[1024,2048]{1,0:T(8,128)(2,1)} %student_hbm.1, f32[8,64,128]{2,1,0:T(8,128)} %broadcast_in_dim.31.weight_ref), custom_call_target="tpu_custom_call" | custom-call | tf_op jit(solution)/shard_map/grad/pallas_call | solution.py:459
  147.7 6.7 %convert_element_type.19 = f32[1024,2048]{1,0:T(8,128)} convert(bf16[1024,2048]{1,0:T(8,128)(2,1)} %grad.1) | non-fusion elementwise | flops 2097152 | bytes 12582912 | tf_op jit(solution)/shard_map/convert_element_type | solution.py:495
  (3 shorter events, 0.0 us)
Async XLA Ops:
  1.1 9.1 %collective-permute-start = (bf16[128,1024]{1,0:T(8,128)(2,1)S(1)}, bf16[128,1024]{1,0:T(8,128)(2,1)S(1)}, u32[]{:S(2)}, u32[]{:S(2)}) collective-permute-start(bf16[128,1024]{1,0:T(8,128)(2,1)S(1)} %multiply_convert_fusion), channel_id=1, source_target_pairs={{0,8},{8,16},{16,24},{1,9},{9,17},{17,25},{2,10},{10,18},{18,26},{... | collective-permute-start | bytes 786440 | tf_op jit(solution)/shard_map/ppermute | solution.py:21
  10.2 0.7 copy-start
